TPU v7x, 32 devices: a whole 2x2x4 slice. The times are simulated.
32 devices in a mesh: section: 4 (over y, core), dp: 8 (over z, x).
Axes of the slice: x: 2, y: 2, z: 4, core: 2. Of those that a mesh axis runs over, the one named last changes fastest.
Arguments:
- fresh_batches: bfloat16 [3, 512, 4096], P(None, 'dp'), may hold values from -6 to 6
- held_states: bfloat16 [4, 512, 4096], P('section', 'dp'), may hold values from -6 to 6
- section_weight: bfloat16 [4, 4096, 4096], P('section', None, 'dp'), may hold values from -0.09375 to 0.09375
- section_gain: float32 [4, 4096], P('section'), may hold values from 0.25 to 1.75
- final_gain: float32 [4096], replicated, may hold values from 0.3 to 3
- cached_pool: bfloat16 [512, 4096], P('dp'), may hold values from -0.09375 to 0.09375
- route: int32 [8, 64], P('dp'), may hold values from 0 to 63, each once within a row
- queries: bfloat16 [256, 4096], P(('section', 'dp')), may hold values from -0.09375 to 0.09375
- shortlist: int32 [256, 128], P(('section', 'dp')), may hold values from 0 to 63
- teacher: float32 [256, 128], P(('section', 'dp')), may hold values from -16 to 300, as said below
Outputs:
- held_out: bfloat16 [4, 512, 4096], P('section', 'dp')
- losses: float32 [256], P(('section', 'dp'))
- query_grad: float32 [256, 4096], P(('section', 'dp'))
- pool_grad: bfloat16 [512, 4096], P('dp')
Inputs may be any that keep to these rules, and one draw needn't show every extreme that they name: `teacher`: reranker scores; on some draws some rows have two entries above the rest.
All inputs are finite; a program needn't handle non-finite values.
Results may differ from a plain program's by a relative error of at most 0.0058.
Values may be sent and summed in bfloat16 or wider, within the bound.
No kernel may reach another device: no remote copies, remote signals or barrier semaphores. Data moves between devices by JAX's collectives and lax.ppermute only.
A program may use at most 64 MiB of HBM per device.

v0:
```python
import jax
import jax.numpy as jnp
from jax import lax
from jax.sharding import PartitionSpec as P

SEQ = 128
TICKS = 3
epsilon = 1e-06
logit_scale = 20.0
AXES = ("section", "dp")


def on_device(
    fresh_batches,
    held_states,
    section_weight,
    section_gain,
    final_gain,
    cached_pool,
    route,
    queries,
    shortlist,
    teacher,
):
    section = lax.axis_index("section")
    sections = lax.axis_size("section")
    dp = lax.axis_index("dp")
    dps = lax.axis_size("dp")
    half = dps // 2
    side, place = (dp % 2, dp // 2)
    weight = section_weight[0]
    gain = section_gain[0]
    width, cols = weight.shape
    tok = held_states.shape[1]
    pair_rows = 2 * tok

    def send(x, hops):
        return lax.ppermute(
            x,
            AXES,
            [(a * dps + i, b * dps + (i ^ flip)) for a, b, flip in hops for i in range(dps)],
        )

    rows = cached_pool.shape[0]
    outbox = jnp.concatenate(
        [
            jnp.take(cached_pool, route[0], axis=0),
            jnp.broadcast_to(route[0].astype(jnp.bfloat16)[:, None], (rows, 128)),
        ],
        axis=1,
    )
    inbox = lax.all_to_all(outbox, "dp", split_axis=0, concat_axis=0, tiled=True)
    owner_queries = lax.all_gather(queries, "section", axis=0, tiled=True)
    gained = (weight.astype(jnp.float32) * gain[:, None]).astype(jnp.bfloat16)
    by_side = gained.reshape(half, 2, cols, cols)
    flips = jnp.where(section == 0, 0, place)
    mine_plain = lax.dynamic_index_in_dim(by_side, side, 1, keepdims=False)
    theirs_plain = lax.dynamic_index_in_dim(by_side, 1 - side, 1, keepdims=False)
    last_full = sections - 1 - TICKS
    theirs_plain = send(theirs_plain, [(a, a, 1) for a in range(sections - 1)])
    order = jnp.arange(half) ^ flips
    inner = half * cols

    def ordered(w):
        return jnp.take(w, order, axis=0).reshape(inner, cols)

    mine_late, theirs_late = (ordered(mine_plain), ordered(theirs_plain))
    if last_full == 0:
        mine_first, theirs_first = (mine_late, theirs_late)
    else:
        mine_first = mine_plain.reshape(inner, cols)
        theirs_first = theirs_plain.reshape(inner, cols)

    def layer(states, mine, theirs, own_at, hops):
        wide = states.astype(jnp.float32)
        square = jnp.sum(wide * wide, axis=-1)
        other_square = send(square, hops)
        other = send(
            jnp.dot(states, theirs, preferred_element_type=jnp.float32).astype(jnp.bfloat16), hops
        )
        own = jnp.dot(states, mine, preferred_element_type=jnp.float32)
        inv_rms = lax.rsqrt((square + other_square) / width + epsilon)
        projected = ((own + other.astype(jnp.float32)) * inv_rms[:, None]).astype(jnp.bfloat16)
        kept = lax.dynamic_slice_in_dim(states, own_at * cols, cols, axis=1).astype(jnp.float32)
        return (kept + jax.nn.silu(projected.astype(jnp.float32))).astype(jnp.bfloat16)

    def token_order(block):
        piled = block.reshape(half, pair_rows, cols)
        return jnp.take(piled, jnp.arange(half) ^ place, axis=0).reshape(block.shape)

    entry = held_states[0]
    for i in range(TICKS - 1):
        entry = jnp.where(section == sections - TICKS + 1 + i, fresh_batches[i], entry)
    used = list(range(last_full + 1)) + list(range(sections - TICKS + 1, sections))
    entry = entry.reshape(tok, half, 2, cols)
    stay = lax.dynamic_index_in_dim(entry, side, 2, keepdims=False).reshape(tok, inner)
    leave = lax.dynamic_index_in_dim(entry, 1 - side, 2, keepdims=False).reshape(tok, inner)
    came = send(leave, [(a, a, 1) for a in used])
    pair = jnp.where(
        side == 0, jnp.concatenate([stay, came], axis=0), jnp.concatenate([came, stay], axis=0)
    )
    piles = [pair] + [send(pair, [(a, a, 2 * k) for a in used]) for k in range(1, half)]
    states = jnp.concatenate(piles, axis=0)
    fresh_states = [send(states, [(sections - TICKS + 1 + i, 0, 0)]) for i in range(TICKS - 1)]
    block = layer(
        states, mine_first, theirs_first, place, [(a, a, 1) for a in range(last_full + 1)]
    )
    block = token_order(block)
    for tick in range(1, TICKS):
        top = last_full + tick
        piles = [send(block, [(a - 1, a, 2 * k) for a in range(1, top + 1)]) for k in range(half)]
        states = jnp.where(section == 0, fresh_states[tick - 1], jnp.concatenate(piles, axis=1))
        block = layer(
            states, mine_late, theirs_late, place - flips, [(a, a, 1) for a in range(top + 1)]
        )
        block = jnp.where(section == 0, token_order(block), block)
    tokens = lax.all_to_all(block, "dp", split_axis=0, concat_axis=1, tiled=True)
    shifted = send(tokens, [(a, a + 1, 0) for a in range(sections - 1)])
    held_out = jnp.where(section == 0, fresh_batches[TICKS - 1], shifted)

    def spread(x):
        return lax.all_to_all(
            jnp.broadcast_to(x[None], (dps, *x.shape)), "dp", split_axis=0, concat_axis=0
        )

    every = SEQ // tok
    ends = spread(held_states[0, tok - 1 :])[every - 1 :: every, 0]
    exits = []
    for tick in range(TICKS):
        wide = ends.astype(jnp.float32)
        inv_rms = lax.rsqrt(jnp.mean(wide * wide, axis=-1, keepdims=True) + epsilon)
        normed = (wide * inv_rms * gain).astype(jnp.bfloat16)
        projected = jnp.dot(normed, weight, preferred_element_type=jnp.float32).astype(jnp.bfloat16)
        kept = lax.dynamic_slice_in_dim(wide, dp * cols, cols, axis=1)
        piece = (kept + jax.nn.silu(projected.astype(jnp.float32))).astype(jnp.bfloat16)
        exits.append(piece)
        if tick < TICKS - 1:
            piece = send(piece, [(a, a + 1, 0) for a in range(sections - 1)])
            ends = jnp.concatenate(list(spread(piece)), axis=1)
    passages = ends.shape[0]
    exit_pieces = lax.all_gather(jnp.concatenate(exits, axis=0), "section", axis=0)[sections - 1]
    exit_rows = jnp.concatenate(list(spread(exit_pieces)), axis=1)
    scaled = exit_rows.astype(jnp.float32) * final_gain
    embedded = (
        scaled * lax.rsqrt(jnp.sum(scaled * scaled, axis=-1, keepdims=True) + epsilon)
    ).astype(jnp.bfloat16)
    per_peer = rows // dps
    source = jnp.arange(rows) // per_peer
    passage = source // every
    is_end = source % every == every - 1
    slot = inbox[:, width].astype(jnp.int32)
    replaced = is_end & (slot < TICKS)
    pick = jnp.where(replaced, slot * passages + passage, -1)
    chosen = (pick[:, None] == jnp.arange(TICKS * passages)).astype(jnp.bfloat16)
    received = jnp.where(
        replaced[:, None],
        jnp.dot(chosen, embedded, preferred_element_type=jnp.float32).astype(jnp.bfloat16),
        inbox[:, :width],
    )
    all_scores = lax.dot_general(
        queries, received, (((1,), (1,)), ((), ())), preferred_element_type=jnp.float32
    )
    listed = shortlist[..., None] == jnp.arange(rows, dtype=jnp.int32)
    student = jnp.sum(jnp.where(listed, all_scores[:, None, :], 0.0), axis=-1) * logit_scale
    student_log = jax.nn.log_softmax(student, axis=-1)
    teacher_log = jax.nn.log_softmax(teacher, axis=-1)
    teacher_prob = jnp.exp(teacher_log)
    losses = jnp.sum(teacher_prob * (teacher_log - student_log), axis=-1)
    logit_grad = logit_scale * (jnp.exp(student_log) - teacher_prob)
    row_grad = jnp.sum(jnp.where(listed, logit_grad[..., None], 0.0), axis=1)
    received_wide = received.astype(jnp.float32)
    owner_grads = lax.all_gather(row_grad, "section", axis=0, tiled=True)
    received_grad = jnp.dot(
        owner_grads.T, owner_queries.astype(jnp.float32), precision=lax.Precision.HIGHEST
    ).astype(jnp.bfloat16)
    query_grad = jnp.dot(row_grad, received_wide, precision=lax.Precision.HIGHEST)
    returned = lax.all_to_all(received_grad, "dp", split_axis=0, concat_axis=0, tiled=True)
    pool_grad = jnp.zeros(returned.shape, jnp.bfloat16).at[route[0]].set(returned)
    return (held_out[None], losses, query_grad, pool_grad)


def solution(mesh):
    return jax.shard_map(
        on_device,
        mesh=mesh,
        in_specs=(
            P(None, "dp", None),
            P("section", "dp", None),
            P("section", None, "dp"),
            P("section", None),
            P(),
            P("dp", None),
            P("dp", None),
            P(("section", "dp"), None),
            P(("section", "dp"), None),
            P(("section", "dp"), None),
        ),
        out_specs=(
            P("section", "dp", None),
            P(("section", "dp")),
            P(("section", "dp"), None),
            P("dp", None),
        ),
        check_vma=False,
    )
```

profile of v0, /device:TPU:0, one launch (start us, length us, event | category | flops | bytes accessed | tf_op | source)
XLA Modules:
  0.0 322.5 jit_solution(15851997710125030554)
XLA Ops:
  3.9 7.3 %all-to-all-start.2 = ((bf16[8,2,2048]{2,1,0:T(2,128)(2,1)}), bf16[8,2,2048]{2,1,0:T(2,128)(2,1)S(1)}, u32[]{:S(2)}, u32[]{:S(2)}) async-start(bf16[8,2,2048]{2,1,0:T(2,128)(2,1)} %reshape.406), calls=%async_computation.2 | async-start | bytes 131072 | tf_op jit(solution)/shard_map/all_to_all | solution.py:122
  17.5 3.9 %collective-permute-start.6 = (bf16[4,512,512]{2,1,0:T(8,128)(2,1)}, bf16[4,512,512]{2,1,0:T(8,128)(2,1)}, u32[]{:S(2)}, u32[]{:S(2)}) collective-permute-start(bf16[4,512,512]{2,1,0:T(8,128)(2,1)} %get-tuple-element.18), channel_id=1, source_target_pairs={{0,1},{1,0},{2,3},{3,2},{4,5},{5,4},{6,7},{7,6},{8,9},{9,8},{10,11... | collective-permute-start | bytes 6291464 | tf_op jit(solution)/shard_map/ppermute | solution.py:38
  41.3 6.0 %all-to-all-start.3 = ((bf16[8,4,512]{2,1,0:T(4,128)(2,1)}), bf16[8,4,512]{2,1,0:T(4,128)(2,1)S(1)}, u32[]{:S(2)}, u32[]{:S(2)}) async-start(bf16[8,4,512]{2,1,0:T(4,128)(2,1)} %broadcast_in_dim.126), calls=%async_computation.3 | async-start | bytes 65536 | tf_op jit(solution)/shard_map/all_to_all | solution.py:122
  47.3 22.6 %all-to-all-done.3 = bf16[8,4,512]{2,1,0:T(4,128)(2,1)S(1)} async-done(((bf16[8,4,512]{2,1,0:T(4,128)(2,1)}), bf16[8,4,512]{2,1,0:T(4,128)(2,1)S(1)}, u32[]{:S(2)}, u32[]{:S(2)}) %all-to-all-start.3) | async-done | bytes 32800 | tf_op jit(solution)/shard_map/all_to_all | solution.py:122
  77.7 5.7 %all-to-all-start.4 = ((bf16[8,4,512]{2,1,0:T(4,128)(2,1)}), bf16[8,4,512]{2,1,0:T(4,128)(2,1)S(1)}, u32[]{:S(2)}, u32[]{:S(2)}) async-start(bf16[8,4,512]{2,1,0:T(4,128)(2,1)} %broadcast_in_dim.127), calls=%async_computation.4 | async-start | bytes 65536 | tf_op jit(solution)/shard_map/all_to_all | solution.py:122
  83.4 5.8 %all_gather.15 = bf16[32,4096]{1,0:T(8,128)(2,1)S(1)} all-gather(bf16[8,4096]{1,0:T(8,128)(2,1)S(1)} %copy-done.10), channel_id=1, replica_groups=mesh['section'=4,'dp'=8] {'section'}, dimensions={0}, use_global_device_ids=true | all-gather | bytes 327680 | tf_op jit(solution)/shard_map/all_gather | solution.py:53
  94.6 4.3 %collective-permute-start.2 = (bf16[128,2048]{1,0:T(8,128)(2,1)S(1)}, bf16[128,2048]{1,0:T(8,128)(2,1)S(1)}, u32[]{:S(2)}, u32[]{:S(2)}) collective-permute-start(bf16[128,2048]{1,0:T(8,128)(2,1)S(1)} %maximum_select_fusion.2), channel_id=1, source_target_pairs={{0,4},{1,5},{2,6},{3,7},{4,0},{5,1},{6,2},{7,3},{16,20},{17,21},{1... | collective-permute-start | bytes 1572872 | tf_op jit(solution)/shard_map/ppermute | solution.py:38
  104.6 5.2 %all-gather.1 = bf16[4,12,512]{2,1,0:T(8,128)(2,1)S(1)} all-gather(bf16[1,12,512]{2,1,0:T(8,128)(2,1)S(1)} %maximum_bitcast_fusion), channel_id=2, replica_groups=mesh['section'=4,'dp'=8] {'section'}, dimensions={0}, use_global_device_ids=true | all-gather | bytes 61440 | tf_op jit(solution)/shard_map/all_gather | solution.py:141
  110.5 5.1 %all-to-all-start.5 = ((bf16[8,12,512]{2,1,0:T(8,128)(2,1)}), bf16[8,12,512]{2,1,0:T(8,128)(2,1)S(1)}, u32[]{:S(2)}, u32[]{:S(2)}) async-start(bf16[8,12,512]{2,1,0:T(8,128)(2,1)} %broadcast_in_dim.129), calls=%async_computation.5 | async-start | bytes 262144 | tf_op jit(solution)/shard_map/all_to_all | solution.py:122
  121.0 3.6 %gather_fusion.2 = bf16[4,512,512]{2,1,0:T(8,128)(2,1)} fusion(bf16[4,512,512]{2,1,0:T(8,128)(2,1)} %collective-permute-done.6, s32[1024]{0:T(1024)S(1)} %pad_clamp_fusion.2), kind=kCustom, calls=%fused_computation.2.clone | custom fusion | bytes 4194320 | tf_op jit(solution)/shard_map/jit(_take)/gather | solution.py:65
  124.6 3.4 %broadcast_select_fusion.1 = (bf16[4,512,512]{2,1,0:T(8,128)(2,1)}, bf16[4,512,512]{2,1,0:T(8,128)(2,1)S(1)}) fusion(bf16[4,512,512]{2,1,0:T(8,128)(2,1)S(1)} %copy-done.1, pred[4]{0:T(512)(128)(4,1)S(1)} %compare_and_fusion.2, bf16[4,512,512]{2,1,0:T(8,128)(2,1)} %gather_fusion.2), kind=kLoop, calls=%fused_computation.28 | loop fusion | flops 2097152 | bytes 8388612 | tf_op jit(solution)/shard_map/jit(_take)/select_n | solution.py:65
  128.0 4.5 %convolution_convert_fusion.4 = bf16[512,512]{1,0:T(8,128)(2,1)} fusion(bf16[512,2048]{1,0:T(8,128)(2,1)} %get-tuple-element.16, bf16[2048,512]{1,0:T(8,128)(2,1)S(1)} %bitcast.209), kind=kOutput, calls=%fused_computation.46 | convolution fusion | flops 1074003968 | bytes 4718592 | tf_op jit(solution)/shard_map/dot_general | solution.py:79
  132.4 3.4 %collective-permute-start.7 = (bf16[512,512]{1,0:T(8,128)(2,1)}, bf16[512,512]{1,0:T(8,128)(2,1)}, u32[]{:S(2)}, u32[]{:S(2)}) collective-permute-start(bf16[512,512]{1,0:T(8,128)(2,1)} %convolution_convert_fusion.4), channel_id=1, source_target_pairs={{0,1},{1,0},{2,3},{3,2},{4,5},{5,4},{6,7},{7,6}} | collective-permute-start | bytes 1572872 | tf_op jit(solution)/shard_map/ppermute | solution.py:38
  135.8 10.5 %all-to-all-start.1 = ((bf16[8,8,4224]{2,1,0:T(8,128)(2,1)}), bf16[8,8,4224]{2,1,0:T(8,128)(2,1)}, u32[]{:S(2)}, u32[]{:S(2)}) async-start(bf16[8,8,4224]{2,1,0:T(8,128)(2,1)} %pad_maximum_fusion.1), calls=%async_computation.1 | async-start | bytes 1081344 | tf_op jit(solution)/shard_map/all_to_all | solution.py:52
  146.9 3.9 %collective-permute-start.8 = (f32[512]{0:T(512)S(1)}, f32[512]{0:T(512)S(1)}, u32[]{:S(2)}, u32[]{:S(2)}) collective-permute-start(f32[512]{0:T(512)S(1)} %get-tuple-element.15), channel_id=1, source_target_pairs={{0,1},{1,0},{2,3},{3,2},{4,5},{5,4},{6,7},{7,6}} | collective-permute-start | bytes 6152 | tf_op jit(solution)/shard_map/ppermute | solution.py:38
  152.6 3.3 %add_convert_fusion.2 = bf16[512,512]{1,0:T(8,128)(2,1)S(1)} fusion(bf16[512,512]{1,0:T(8,128)(2,1)} %collective-permute-done.7, bf16[512,2048]{1,0:T(8,128)(2,1)} %get-tuple-element.16, bf16[2048,512]{1,0:T(8,128)(2,1)S(1)} %bitcast.207, f32[512]{0:T(512)S(1)} %add_rsqrt_fusion.2, s32[]{:T(128)S(6)} %select_n.203), kind=kOutput, calls=%fused_computation.65 | convolution fusion | flops 1076887552 | bytes 5769220 | tf_op jit(solution)/shard_map/dot_general | solution.py:81
  165.3 5.0 %collective-permute-done.11 = bf16[512,512]{1,0:T(8,128)(2,1)S(1)} collective-permute-done((bf16[512,512]{1,0:T(8,128)(2,1)S(1)}, bf16[512,512]{1,0:T(8,128)(2,1)S(1)}, u32[]{:S(2)}, u32[]{:S(2)}) %collective-permute-start.11) | collective-permute-done | bytes 524320 | tf_op jit(solution)/shard_map/ppermute | solution.py:38
  170.3 5.6 %collective-permute-done.12 = bf16[512,512]{1,0:T(8,128)(2,1)S(1)} collective-permute-done((bf16[512,512]{1,0:T(8,128)(2,1)S(1)}, bf16[512,512]{1,0:T(8,128)(2,1)S(1)}, u32[]{:S(2)}, u32[]{:S(2)}) %collective-permute-start.12) | collective-permute-done | bytes 524320 | tf_op jit(solution)/shard_map/ppermute | solution.py:38
  179.5 3.9 %collective-permute-start.13 = (bf16[512,512]{1,0:T(8,128)(2,1)S(1)}, bf16[512,512]{1,0:T(8,128)(2,1)S(1)}, u32[]{:S(2)}, u32[]{:S(2)}) collective-permute-start(bf16[512,512]{1,0:T(8,128)(2,1)S(1)} %convolution_convert_fusion.3), channel_id=1, source_target_pairs={{0,1},{1,0},{2,3},{3,2},{4,5},{5,4},{6,7},{7,6},{8,9},{9,8},{10,11... | collective-permute-start | bytes 1572872 | tf_op jit(solution)/shard_map/ppermute | solution.py:38
  186.6 7.2 %collective-permute-done.14 = f32[512]{0:T(512)S(1)} collective-permute-done((f32[512]{0:T(512)S(1)}, f32[512]{0:T(512)S(1)}, u32[]{:S(2)}, u32[]{:S(2)}) %collective-permute-start.14) | collective-permute-done | bytes 2080 | tf_op jit(solution)/shard_map/ppermute | solution.py:38
  197.9 4.5 %collective-permute-start.15 = (bf16[512,512]{1,0:T(8,128)(2,1)S(1)}, bf16[512,512]{1,0:T(8,128)(2,1)S(1)}, u32[]{:S(2)}, u32[]{:S(2)}) collective-permute-start(bf16[512,512]{1,0:T(8,128)(2,1)S(1)} %bitcast_select_fusion.2), channel_id=1, source_target_pairs={{0,8},{1,9},{2,10},{3,11},{4,12},{5,13},{6,14},{7,15},{8,16},{9,17... | collective-permute-start | bytes 1572872 | tf_op jit(solution)/shard_map/ppermute | solution.py:38
  202.5 10.1 %collective-permute-start.16 = (bf16[512,512]{1,0:T(8,128)(2,1)S(1)}, bf16[512,512]{1,0:T(8,128)(2,1)S(1)}, u32[]{:S(2)}, u32[]{:S(2)}) collective-permute-start(bf16[512,512]{1,0:T(8,128)(2,1)S(1)} %bitcast_select_fusion.2), channel_id=1, source_target_pairs={{0,10},{1,11},{2,8},{3,9},{4,14},{5,15},{6,12},{7,13},{8,18},{9,19... | collective-permute-start | bytes 1572872 | tf_op jit(solution)/shard_map/ppermute | solution.py:38
  215.5 9.4 %collective-permute-done.16 = bf16[512,512]{1,0:T(8,128)(2,1)S(1)} collective-permute-done((bf16[512,512]{1,0:T(8,128)(2,1)S(1)}, bf16[512,512]{1,0:T(8,128)(2,1)S(1)}, u32[]{:S(2)}, u32[]{:S(2)}) %collective-permute-start.16) | collective-permute-done | bytes 524320 | tf_op jit(solution)/shard_map/ppermute | solution.py:38
  224.9 8.7 %collective-permute-done.17 = bf16[512,512]{1,0:T(8,128)(2,1)S(1)} collective-permute-done((bf16[512,512]{1,0:T(8,128)(2,1)S(1)}, bf16[512,512]{1,0:T(8,128)(2,1)S(1)}, u32[]{:S(2)}, u32[]{:S(2)}) %collective-permute-start.17) | collective-permute-done | bytes 524320 | tf_op jit(solution)/shard_map/ppermute | solution.py:38
  233.6 5.6 %collective-permute-done.18 = bf16[512,512]{1,0:T(8,128)(2,1)S(1)} collective-permute-done((bf16[512,512]{1,0:T(8,128)(2,1)S(1)}, bf16[512,512]{1,0:T(8,128)(2,1)S(1)}, u32[]{:S(2)}, u32[]{:S(2)}) %collective-permute-start.18) | collective-permute-done | bytes 524320 | tf_op jit(solution)/shard_map/ppermute | solution.py:38
  241.6 3.6 %collective-permute-start.19 = (bf16[512,512]{1,0:T(8,128)(2,1)S(1)}, bf16[512,512]{1,0:T(8,128)(2,1)S(1)}, u32[]{:S(2)}, u32[]{:S(2)}) collective-permute-start(bf16[512,512]{1,0:T(8,128)(2,1)S(1)} %convolution_convert_fusion.2), channel_id=1, source_target_pairs={{0,1},{1,0},{2,3},{3,2},{4,5},{5,4},{6,7},{7,6},{8,9},{9,8},{10,11... | collective-permute-start | bytes 1572872 | tf_op jit(solution)/shard_map/ppermute | solution.py:38
  252.7 3.9 %add_convert_fusion = bf16[512,512]{1,0:T(8,128)(2,1)S(1)} fusion(f32[512]{0:T(512)S(1)} %add_rsqrt_fusion, bf16[512,512]{1,0:T(8,128)(2,1)S(1)} %collective-permute-done.19, bf16[512,2048]{1,0:T(8,128)(2,1)} %copy-done.2, bf16[2048,512]{1,0:T(8,128)(2,1)} %bitcast.206, s32[]{:T(128)S(6)} %select_n.206), kind=kOutput, calls=%fused_computation.63 | convolution fusion | flops 1076887552 | bytes 5769220 | tf_op jit(solution)/shard_map/dot_general | solution.py:81
  258.2 27.3 %all-to-all-start = ((bf16[8,64,512]{2,1,0:T(8,128)(2,1)}), bf16[8,64,512]{2,1,0:T(8,128)(2,1)S(1)}, u32[]{:S(2)}, u32[]{:S(2)}) async-start(bf16[8,64,512]{2,1,0:T(8,128)(2,1)} %bitcast.12), calls=%async_computation | async-start | bytes 1048576 | tf_op jit(solution)/shard_map/all_to_all | solution.py:117
  287.0 5.2 %all_gather.14 = f32[32,64]{1,0:T(8,128)S(1)} all-gather(f32[8,64]{1,0:T(8,128)S(1)} %select_reduce_fusion), channel_id=1, replica_groups=mesh['section'=4,'dp'=8] {'section'}, dimensions={0}, use_global_device_ids=true | all-gather | bytes 10240 | tf_op jit(solution)/shard_map/all_gather | solution.py:172
  293.6 6.4 %all-to-all-done = bf16[8,64,512]{2,1,0:T(8,128)(2,1)S(1)} async-done(((bf16[8,64,512]{2,1,0:T(8,128)(2,1)}), bf16[8,64,512]{2,1,0:T(8,128)(2,1)S(1)}, u32[]{:S(2)}, u32[]{:S(2)}) %all-to-all-start) | async-done | bytes 524320 | tf_op jit(solution)/shard_map/all_to_all | solution.py:117
  300.1 3.6 %all-to-all-start.6 = ((bf16[8,8,4096]{2,1,0:T(8,128)(2,1)}), bf16[8,8,4096]{2,1,0:T(8,128)(2,1)S(1)}, u32[]{:S(2)}, u32[]{:S(2)}) async-start(bf16[8,8,4096]{2,1,0:T(8,128)(2,1)} %fusion.2), calls=%async_computation.6 | async-start | bytes 1048576 | tf_op jit(solution)/shard_map/all_to_all | solution.py:177
  306.4 12.0 %all-to-all-done.6 = bf16[8,8,4096]{2,1,0:T(8,128)(2,1)S(1)} async-done(((bf16[8,8,4096]{2,1,0:T(8,128)(2,1)}), bf16[8,8,4096]{2,1,0:T(8,128)(2,1)S(1)}, u32[]{:S(2)}, u32[]{:S(2)}) %all-to-all-start.6) | async-done | bytes 524320 | tf_op jit(solution)/shard_map/all_to_all | solution.py:177
  (202 shorter events, 100.5 us)
Async XLA Ops:
  0.6 32.3 %copy-start = (bf16[64,4096]{1,0:T(8,128)(2,1)S(1)}, bf16[64,4096]{1,0:T(8,128)(2,1)}, u32[]{:S(2)}) copy-start(bf16[64,4096]{1,0:T(8,128)(2,1)} %param.20) | copy-start | bytes 1572868
  3.9 31.4 %all-to-all-start.2 = ((bf16[8,2,2048]{2,1,0:T(2,128)(2,1)}), bf16[8,2,2048]{2,1,0:T(2,128)(2,1)S(1)}, u32[]{:S(2)}, u32[]{:S(2)}) async-start(bf16[8,2,2048]{2,1,0:T(2,128)(2,1)} %reshape.406), calls=%async_computation.2 | async-start | bytes 131072 | tf_op jit(solution)/shard_map/all_to_all | solution.py:122
  17.5 103.5 %collective-permute-start.6 = (bf16[4,512,512]{2,1,0:T(8,128)(2,1)}, bf16[4,512,512]{2,1,0:T(8,128)(2,1)}, u32[]{:S(2)}, u32[]{:S(2)}) collective-permute-start(bf16[4,512,512]{2,1,0:T(8,128)(2,1)} %get-tuple-element.18), channel_id=1, source_target_pairs={{0,1},{1,0},{2,3},{3,2},{4,5},{5,4},{6,7},{7,6},{8,9},{9,8},{10,11... | collective-permute-start | bytes 6291464 | tf_op jit(solution)/shard_map/ppermute | solution.py:38
  29.0 61.4 %collective-permute-start = (bf16[64,2048]{1,0:T(8,128)(2,1)}, bf16[64,2048]{1,0:T(8,128)(2,1)}, u32[]{:S(2)}, u32[]{:S(2)}) collective-permute-start(bf16[64,2048]{1,0:T(8,128)(2,1)} %bitcast.57), channel_id=1, source_target_pairs={{0,1},{1,0},{2,3},{3,2},{4,5},{5,4},{6,7},{7,6},{16,17},{17,16},{1... | collective-permute-start | bytes 786440 | tf_op jit(solution)/shard_map/ppermute | solution.py:38
  38.6 2.1 collective-permute-start.22
  41.3 28.6 %all-to-all-start.3 = ((bf16[8,4,512]{2,1,0:T(4,128)(2,1)}), bf16[8,4,512]{2,1,0:T(4,128)(2,1)S(1)}, u32[]{:S(2)}, u32[]{:S(2)}) async-start(bf16[8,4,512]{2,1,0:T(4,128)(2,1)} %broadcast_in_dim.126), calls=%async_computation.3 | async-start | bytes 65536 | tf_op jit(solution)/shard_map/all_to_all | solution.py:122
  73.1 4.0 %collective-permute-start.23 = (bf16[4,512]{1,0:T(4,128)(2,1)S(1)}, bf16[4,512]{1,0:T(4,128)(2,1)S(1)}, u32[]{:S(2)}, u32[]{:S(2)}) collective-permute-start(bf16[4,512]{1,0:T(4,128)(2,1)S(1)} %fusion.81), channel_id=1, source_target_pairs={{0,8},{1,9},{2,10},{3,11},{4,12},{5,13},{6,14},{7,15},{8,16},{9,17... | collective-permute-start | bytes 12296 | tf_op jit(solution)/shard_map/ppermute | solution.py:38
  77.7 12.4 %all-to-all-start.4 = ((bf16[8,4,512]{2,1,0:T(4,128)(2,1)}), bf16[8,4,512]{2,1,0:T(4,128)(2,1)S(1)}, u32[]{:S(2)}, u32[]{:S(2)}) async-start(bf16[8,4,512]{2,1,0:T(4,128)(2,1)} %broadcast_in_dim.127), calls=%async_computation.4 | async-start | bytes 65536 | tf_op jit(solution)/shard_map/all_to_all | solution.py:122
  91.5 24.1 %collective-permute-start.1 = (bf16[128,2048]{1,0:T(8,128)(2,1)S(1)}, bf16[128,2048]{1,0:T(8,128)(2,1)S(1)}, u32[]{:S(2)}, u32[]{:S(2)}) collective-permute-start(bf16[128,2048]{1,0:T(8,128)(2,1)S(1)} %maximum_select_fusion.2), channel_id=1, source_target_pairs={{0,2},{1,3},{2,0},{3,1},{4,6},{5,7},{6,4},{7,5},{16,18},{17,19},{1... | collective-permute-start | bytes 1572872 | tf_op jit(solution)/shard_map/ppermute | solution.py:38
  94.6 23.3 %collective-permute-start.2 = (bf16[128,2048]{1,0:T(8,128)(2,1)S(1)}, bf16[128,2048]{1,0:T(8,128)(2,1)S(1)}, u32[]{:S(2)}, u32[]{:S(2)}) collective-permute-start(bf16[128,2048]{1,0:T(8,128)(2,1)S(1)} %maximum_select_fusion.2), channel_id=1, source_target_pairs={{0,4},{1,5},{2,6},{3,7},{4,0},{5,1},{6,2},{7,3},{16,20},{17,21},{1... | collective-permute-start | bytes 1572872 | tf_op jit(solution)/shard_map/ppermute | solution.py:38
  98.8 19.0 %collective-permute-start.3 = (bf16[128,2048]{1,0:T(8,128)(2,1)S(1)}, bf16[128,2048]{1,0:T(8,128)(2,1)S(1)}, u32[]{:S(2)}, u32[]{:S(2)}) collective-permute-start(bf16[128,2048]{1,0:T(8,128)(2,1)S(1)} %maximum_select_fusion.2), channel_id=1, source_target_pairs={{0,6},{1,7},{2,4},{3,5},{4,2},{5,3},{6,0},{7,1},{16,22},{17,23},{1... | collective-permute-start | bytes 1572872 | tf_op jit(solution)/shard_map/ppermute | solution.py:38
  110.5 25.3 %all-to-all-start.5 = ((bf16[8,12,512]{2,1,0:T(8,128)(2,1)}), bf16[8,12,512]{2,1,0:T(8,128)(2,1)S(1)}, u32[]{:S(2)}, u32[]{:S(2)}) async-start(bf16[8,12,512]{2,1,0:T(8,128)(2,1)} %broadcast_in_dim.129), calls=%async_computation.5 | async-start | bytes 262144 | tf_op jit(solution)/shard_map/all_to_all | solution.py:122
  119.4 44.5 %collective-permute-start.5 = (bf16[512,2048]{1,0:T(8,128)(2,1)}, bf16[512,2048]{1,0:T(8,128)(2,1)}, u32[]{:S(2)}, u32[]{:S(2)}) collective-permute-start(bf16[512,2048]{1,0:T(8,128)(2,1)} %get-tuple-element.16), channel_id=1, source_target_pairs={{16,0},{17,1},{18,2},{19,3},{20,4},{21,5},{22,6},{23,7}} | collective-permute-start | bytes 6291464 | tf_op jit(solution)/shard_map/ppermute | solution.py:38
  132.4 20.1 %collective-permute-start.7 = (bf16[512,512]{1,0:T(8,128)(2,1)}, bf16[512,512]{1,0:T(8,128)(2,1)}, u32[]{:S(2)}, u32[]{:S(2)}) collective-permute-start(bf16[512,512]{1,0:T(8,128)(2,1)} %convolution_convert_fusion.4), channel_id=1, source_target_pairs={{0,1},{1,0},{2,3},{3,2},{4,5},{5,4},{6,7},{7,6}} | collective-permute-start | bytes 1572872 | tf_op jit(solution)/shard_map/ppermute | solution.py:38
  135.8 109.3 %all-to-all-start.1 = ((bf16[8,8,4224]{2,1,0:T(8,128)(2,1)}), bf16[8,8,4224]{2,1,0:T(8,128)(2,1)}, u32[]{:S(2)}, u32[]{:S(2)}) async-start(bf16[8,8,4224]{2,1,0:T(8,128)(2,1)} %pad_maximum_fusion.1), calls=%async_computation.1 | async-start | bytes 1081344 | tf_op jit(solution)/shard_map/all_to_all | solution.py:52
  146.9 5.7 %collective-permute-start.8 = (f32[512]{0:T(512)S(1)}, f32[512]{0:T(512)S(1)}, u32[]{:S(2)}, u32[]{:S(2)}) collective-permute-start(f32[512]{0:T(512)S(1)} %get-tuple-element.15), channel_id=1, source_target_pairs={{0,1},{1,0},{2,3},{3,2},{4,5},{5,4},{6,7},{7,6}} | collective-permute-start | bytes 6152 | tf_op jit(solution)/shard_map/ppermute | solution.py:38
  156.6 8.6 %collective-permute-start.10 = (bf16[512,512]{1,0:T(8,128)(2,1)S(1)}, bf16[512,512]{1,0:T(8,128)(2,1)S(1)}, u32[]{:S(2)}, u32[]{:S(2)}) collective-permute-start(bf16[512,512]{1,0:T(8,128)(2,1)S(1)} %bitcast.216), channel_id=1, source_target_pairs={{0,10},{1,11},{2,8},{3,9},{4,14},{5,15},{6,12},{7,13}} | collective-permute-start | bytes 1572872 | tf_op jit(solution)/shard_map/ppermute | solution.py:38
  158.0 12.3 %collective-permute-start.11 = (bf16[512,512]{1,0:T(8,128)(2,1)S(1)}, bf16[512,512]{1,0:T(8,128)(2,1)S(1)}, u32[]{:S(2)}, u32[]{:S(2)}) collective-permute-start(bf16[512,512]{1,0:T(8,128)(2,1)S(1)} %bitcast.217), channel_id=1, source_target_pairs={{0,12},{1,13},{2,14},{3,15},{4,8},{5,9},{6,10},{7,11}} | collective-permute-start | bytes 1572872 | tf_op jit(solution)/shard_map/ppermute | solution.py:38
  159.3 16.6 %collective-permute-start.12 = (bf16[512,512]{1,0:T(8,128)(2,1)S(1)}, bf16[512,512]{1,0:T(8,128)(2,1)S(1)}, u32[]{:S(2)}, u32[]{:S(2)}) collective-permute-start(bf16[512,512]{1,0:T(8,128)(2,1)S(1)} %bitcast.218), channel_id=1, source_target_pairs={{0,14},{1,15},{2,12},{3,13},{4,10},{5,11},{6,8},{7,9}} | collective-permute-start | bytes 1572872 | tf_op jit(solution)/shard_map/ppermute | solution.py:38
  160.6 15.3 %collective-permute-start.9 = (bf16[512,512]{1,0:T(8,128)(2,1)S(1)}, bf16[512,512]{1,0:T(8,128)(2,1)S(1)}, u32[]{:S(2)}, u32[]{:S(2)}) collective-permute-start(bf16[512,512]{1,0:T(8,128)(2,1)S(1)} %bitcast.219), channel_id=1, source_target_pairs={{0,8},{1,9},{2,10},{3,11},{4,12},{5,13},{6,14},{7,15}} | collective-permute-start | bytes 1572872 | tf_op jit(solution)/shard_map/ppermute | solution.py:38
  163.9 51.6 %collective-permute-start.4 = (bf16[512,2048]{1,0:T(8,128)(2,1)}, bf16[512,2048]{1,0:T(8,128)(2,1)S(1)}, u32[]{:S(2)}, u32[]{:S(2)}) collective-permute-start(bf16[512,2048]{1,0:T(8,128)(2,1)} %get-tuple-element.16), channel_id=1, source_target_pairs={{24,0},{25,1},{26,2},{27,3},{28,4},{29,5},{30,6},{31,7}} | collective-permute-start | bytes 6291464 | tf_op jit(solution)/shard_map/ppermute | solution.py:38
  179.5 14.3 %collective-permute-start.13 = (bf16[512,512]{1,0:T(8,128)(2,1)S(1)}, bf16[512,512]{1,0:T(8,128)(2,1)S(1)}, u32[]{:S(2)}, u32[]{:S(2)}) collective-permute-start(bf16[512,512]{1,0:T(8,128)(2,1)S(1)} %convolution_convert_fusion.3), channel_id=1, source_target_pairs={{0,1},{1,0},{2,3},{3,2},{4,5},{5,4},{6,7},{7,6},{8,9},{9,8},{10,11... | collective-permute-start | bytes 1572872 | tf_op jit(solution)/shard_map/ppermute | solution.py:38
  184.0 9.7 %collective-permute-start.14 = (f32[512]{0:T(512)S(1)}, f32[512]{0:T(512)S(1)}, u32[]{:S(2)}, u32[]{:S(2)}) collective-permute-start(f32[512]{0:T(512)S(1)} %get-tuple-element.13), channel_id=1, source_target_pairs={{0,1},{1,0},{2,3},{3,2},{4,5},{5,4},{6,7},{7,6},{8,9},{9,8},{10,11... | collective-permute-start | bytes 6152 | tf_op jit(solution)/shard_map/ppermute | solution.py:38
  197.9 17.5 %collective-permute-start.15 = (bf16[512,512]{1,0:T(8,128)(2,1)S(1)}, bf16[512,512]{1,0:T(8,128)(2,1)S(1)}, u32[]{:S(2)}, u32[]{:S(2)}) collective-permute-start(bf16[512,512]{1,0:T(8,128)(2,1)S(1)} %bitcast_select_fusion.2), channel_id=1, source_target_pairs={{0,8},{1,9},{2,10},{3,11},{4,12},{5,13},{6,14},{7,15},{8,16},{9,17... | collective-permute-start | bytes 1572872 | tf_op jit(solution)/shard_map/ppermute | solution.py:38
  202.5 22.4 %collective-permute-start.16 = (bf16[512,512]{1,0:T(8,128)(2,1)S(1)}, bf16[512,512]{1,0:T(8,128)(2,1)S(1)}, u32[]{:S(2)}, u32[]{:S(2)}) collective-permute-start(bf16[512,512]{1,0:T(8,128)(2,1)S(1)} %bitcast_select_fusion.2), channel_id=1, source_target_pairs={{0,10},{1,11},{2,8},{3,9},{4,14},{5,15},{6,12},{7,13},{8,18},{9,19... | collective-permute-start | bytes 1572872 | tf_op jit(solution)/shard_map/ppermute | solution.py:38
  212.5 21.0 %collective-permute-start.17 = (bf16[512,512]{1,0:T(8,128)(2,1)S(1)}, bf16[512,512]{1,0:T(8,128)(2,1)S(1)}, u32[]{:S(2)}, u32[]{:S(2)}) collective-permute-start(bf16[512,512]{1,0:T(8,128)(2,1)S(1)} %bitcast_select_fusion.2), channel_id=1, source_target_pairs={{0,12},{1,13},{2,14},{3,15},{4,8},{5,9},{6,10},{7,11},{8,20},{9,21... | collective-permute-start | bytes 1572872 | tf_op jit(solution)/shard_map/ppermute | solution.py:38
  213.9 25.3 %collective-permute-start.18 = (bf16[512,512]{1,0:T(8,128)(2,1)S(1)}, bf16[512,512]{1,0:T(8,128)(2,1)S(1)}, u32[]{:S(2)}, u32[]{:S(2)}) collective-permute-start(bf16[512,512]{1,0:T(8,128)(2,1)S(1)} %bitcast_select_fusion.2), channel_id=1, source_target_pairs={{0,14},{1,15},{2,12},{3,13},{4,10},{5,11},{6,8},{7,9},{8,22},{9,23... | collective-permute-start | bytes 1572872 | tf_op jit(solution)/shard_map/ppermute | solution.py:38
  241.6 11.1 %collective-permute-start.19 = (bf16[512,512]{1,0:T(8,128)(2,1)S(1)}, bf16[512,512]{1,0:T(8,128)(2,1)S(1)}, u32[]{:S(2)}, u32[]{:S(2)}) collective-permute-start(bf16[512,512]{1,0:T(8,128)(2,1)S(1)} %convolution_convert_fusion.2), channel_id=1, source_target_pairs={{0,1},{1,0},{2,3},{3,2},{4,5},{5,4},{6,7},{7,6},{8,9},{9,8},{10,11... | collective-permute-start | bytes 1572872 | tf_op jit(solution)/shard_map/ppermute | solution.py:38
  246.1 6.5 %collective-permute-start.20 = (f32[512]{0:T(512)S(1)}, f32[512]{0:T(512)S(1)}, u32[]{:S(2)}, u32[]{:S(2)}) collective-permute-start(f32[512]{0:T(512)S(1)} %get-tuple-element.11), channel_id=1, source_target_pairs={{0,1},{1,0},{2,3},{3,2},{4,5},{5,4},{6,7},{7,6},{8,9},{9,8},{10,11... | collective-permute-start | bytes 6152 | tf_op jit(solution)/shard_map/ppermute | solution.py:38
  258.2 41.9 %all-to-all-start = ((bf16[8,64,512]{2,1,0:T(8,128)(2,1)}), bf16[8,64,512]{2,1,0:T(8,128)(2,1)S(1)}, u32[]{:S(2)}, u32[]{:S(2)}) async-start(bf16[8,64,512]{2,1,0:T(8,128)(2,1)} %bitcast.12), calls=%async_computation | async-start | bytes 1048576 | tf_op jit(solution)/shard_map/all_to_all | solution.py:117
  300.1 18.3 %all-to-all-start.6 = ((bf16[8,8,4096]{2,1,0:T(8,128)(2,1)}), bf16[8,8,4096]{2,1,0:T(8,128)(2,1)S(1)}, u32[]{:S(2)}, u32[]{:S(2)}) async-start(bf16[8,8,4096]{2,1,0:T(8,128)(2,1)} %fusion.2), calls=%async_computation.6 | async-start | bytes 1048576 | tf_op jit(solution)/shard_map/all_to_all | solution.py:177
  303.7 16.8 %collective-permute-start.21 = (bf16[64,4096]{1,0:T(8,128)(2,1)S(1)}, bf16[64,4096]{1,0:T(8,128)(2,1)S(1)}, u32[]{:S(2)}, u32[]{:S(2)}) collective-permute-start(bf16[64,4096]{1,0:T(8,128)(2,1)S(1)} %bitcast.215), channel_id=1, source_target_pairs={{0,8},{1,9},{2,10},{3,11},{4,12},{5,13},{6,14},{7,15},{8,16},{9,17... | collective-permute-start | bytes 1572872 | tf_op jit(solution)/shard_map/ppermute | solution.py:38
  (23 other events, 305.9 us)
where the time goes:
time: 324 us; the launch traced here: 322 us
  starting transfers between devices  130 us (40%)
  waiting for transfers between devices  90.5 us (28%)
  local copies, waits for them, and re-layouts  29.6 us (9%)
  matrix products  28.3 us (9%)
  other arithmetic  26.2 us (8%)
  blocking collectives  16.2 us (5%)
    ppermute x24, starting transfers between devices, send(): lax.ppermute(x, AXES, [(a * dps + i, b * dps + (i ^ flip)) for a, b, flip...  64.7 us
    ppermute x24, waiting for transfers between devices, send(): lax.ppermute(x, AXES, [(a * dps + i, b * dps + (i ^ flip)) for a, b, flip...  48.6 us
    all_to_all x1, starting transfers between devices, on_device(): lax.all_to_all(block, 'dp', split_axis=0, concat_axis=1, tiled=True)  27.3 us
    all_to_all x4, starting transfers between devices, spread(): lax.all_to_all(jnp.broadcast_to(x[None], (dps, *x.shape)), 'dp', split_ax...  24.1 us
    all_to_all x4, waiting for transfers between devices, spread(): lax.all_to_all(jnp.broadcast_to(x[None], (dps, *x.shape)), 'dp', split_ax...  23.5 us
    all_to_all x1, waiting for transfers between devices, on_device(): lax.all_to_all(received_grad, 'dp', split_axis=0, concat_axis=0, tiled=True)  12 us
    all_to_all x1, starting transfers between devices, on_device(): lax.all_to_all(outbox, 'dp', split_axis=0, concat_axis=0, tiled=True)  10.5 us
    dot_general x3, matrix products, layer(): own = jnp.dot(states, mine, preferred_element_type=jnp.float32)  8.69 us
  transfers between devices with their start and end apart: 31, of which 15 were waited for; matrix products, arithmetic and copies ran while one was open for 23% of the time, Pallas kernels for 0%

commit v1 on v0

--- a/solution.py
+++ b/solution.py
@@ -22,6 +22,25 @@
     shortlist,
     teacher,
 ):
+
+    def _time_orders(x_local):
+        axis_key = "dp"
+        d_next = lax.axis_index(axis_key)
+        block_next = lax.axis_size(axis_key)
+        val2, opened = (block_next, d_next)
+        all_values = list(x_local.shape)
+        b_next = x_local.shape[0] // val2
+        all_values[0] = b_next
+        mixed_arr = all_values[1]
+        all_values[1] = mixed_arr * val2
+        v_next = jnp.zeros(all_values, x_local.dtype)
+        for h in range(val2):
+            tmp = lax.dynamic_slice_in_dim(x_local, (opened ^ h) * b_next, b_next, axis=0)
+            if h:
+                tmp = lax.ppermute(tmp, axis_key, [(ii, ii ^ h) for ii in range(val2)])
+            v_next = lax.dynamic_update_slice_in_dim(v_next, tmp, (opened ^ h) * mixed_arr, axis=1)
+        return v_next
+
     section = lax.axis_index("section")
     sections = lax.axis_size("section")
     dp = lax.axis_index("dp")
@@ -114,7 +133,7 @@
             states, mine_late, theirs_late, place - flips, [(a, a, 1) for a in range(top + 1)]
         )
         block = jnp.where(section == 0, token_order(block), block)
-    tokens = lax.all_to_all(block, "dp", split_axis=0, concat_axis=1, tiled=True)
+    tokens = _time_orders(block)
     shifted = send(tokens, [(a, a + 1, 0) for a in range(sections - 1)])
     held_out = jnp.where(section == 0, fresh_batches[TICKS - 1], shifted)
 

time: 324 us -> 338 us (1.043); the launches traced: 322 us -> 333 us
  blocking collectives: 16.2 us -> 28.1 us
  waiting for transfers between devices: 90.5 us -> 94.5 us
  local copies, waits for them, and re-layouts: 29.6 us -> 25.8 us
    all_to_all x1 -> x0, starting transfers between devices: 27.3 us -> none  [on_device(): lax.all_to_all(block, 'dp', split_axis=0, concat_axis=1, tiled=True)]
    ppermute x0 -> x7, starting transfers between devices: none -> 15.7 us  [_time_orders(): tmp = lax.ppermute(tmp, axis_key, [(ii, ii ^ h) for ii in range(val2)])]
    all_to_all x1, waiting for transfers between devices: 12 us -> 0.01 us  [on_device(): lax.all_to_all(received_grad, 'dp', split_axis=0, concat_axis=0, tiled=True)]
    all_gather x1, blocking collectives: 5.21 us -> 17 us  [on_device(): owner_grads = lax.all_gather(row_grad, 'section', axis=0, tiled=True)]
    ppermute x24, waiting for transfers between devices: 48.6 us -> 59.9 us  [send(): lax.ppermute(x, AXES, [(a * dps + i, b * dps + (i ^ flip)) for a, b, flip...]
    ppermute x0 -> x7, waiting for transfers between devices: none -> 10.7 us  [_time_orders(): tmp = lax.ppermute(tmp, axis_key, [(ii, ii ^ h) for ii in range(val2)])]
    all_to_all x1, starting transfers between devices: 3.64 us -> 12.7 us  [on_device(): lax.all_to_all(received_grad, 'dp', split_axis=0, concat_axis=0, tiled=True)]
    all_to_all x1 -> x0, waiting for transfers between devices: 6.43 us -> none  [on_device(): lax.all_to_all(block, 'dp', split_axis=0, concat_axis=1, tiled=True)]
  transfers between devices with their start and end apart: 31 -> 37, of which waited for: 15 -> 14; matrix products, arithmetic and copies ran while one was open for 23% -> 21% of each run, Pallas kernels for 0% -> 0%
where the time goes in v1:
time: 338 us; the launch traced here: 333 us
  starting transfers between devices  129 us (38%)
  waiting for transfers between devices  94.5 us (28%)
  matrix products  29.8 us (9%)
  blocking collectives  28.1 us (8%)
  local copies, waits for them, and re-layouts  25.8 us (8%)
  other arithmetic  24 us (7%)
    ppermute x24, starting transfers between devices, send(): lax.ppermute(x, AXES, [(a * dps + i, b * dps + (i ^ flip)) for a, b, flip...  70.7 us
    ppermute x24, waiting for transfers between devices, send(): lax.ppermute(x, AXES, [(a * dps + i, b * dps + (i ^ flip)) for a, b, flip...  59.9 us
    all_to_all x4, starting transfers between devices, spread(): lax.all_to_all(jnp.broadcast_to(x[None], (dps, *x.shape)), 'dp', split_ax...  24.1 us
    all_to_all x4, waiting for transfers between devices, spread(): lax.all_to_all(jnp.broadcast_to(x[None], (dps, *x.shape)), 'dp', split_ax...  23.9 us
    all_gather x1, blocking collectives, on_device(): owner_grads = lax.all_gather(row_grad, 'section', axis=0, tiled=True)  17 us
    ppermute x7, starting transfers between devices, _time_orders(): tmp = lax.ppermute(tmp, axis_key, [(ii, ii ^ h) for ii in range(val2)])  15.7 us
    all_to_all x1, starting transfers between devices, on_device(): lax.all_to_all(received_grad, 'dp', split_axis=0, concat_axis=0, tiled=True)  12.7 us
    ppermute x7, waiting for transfers between devices, _time_orders(): tmp = lax.ppermute(tmp, axis_key, [(ii, ii ^ h) for ii in range(val2)])  10.7 us
  transfers between devices with their start and end apart: 37, of which 14 were waited for; matrix products, arithmetic and copies ran while one was open for 21% of the time, Pallas kernels for 0%

profile of v1, /device:TPU:0, one launch (start us, length us, event | category | flops | bytes accessed | tf_op | source)
XLA Modules:
  0.0 333.0 jit_solution(4056253683199677501)
XLA Ops:
  3.9 7.3 %all-to-all-start.1 = ((bf16[8,2,2048]{2,1,0:T(2,128)(2,1)}), bf16[8,2,2048]{2,1,0:T(2,128)(2,1)S(1)}, u32[]{:S(2)}, u32[]{:S(2)}) async-start(bf16[8,2,2048]{2,1,0:T(2,128)(2,1)} %reshape.403), calls=%async_computation.1 | async-start | bytes 131072 | tf_op jit(solution)/shard_map/all_to_all | solution.py:141
  17.5 3.9 %collective-permute-start.6 = (bf16[4,512,512]{2,1,0:T(8,128)(2,1)}, bf16[4,512,512]{2,1,0:T(8,128)(2,1)}, u32[]{:S(2)}, u32[]{:S(2)}) collective-permute-start(bf16[4,512,512]{2,1,0:T(8,128)(2,1)} %get-tuple-element.18), channel_id=1, source_target_pairs={{0,1},{1,0},{2,3},{3,2},{4,5},{5,4},{6,7},{7,6},{8,9},{9,8},{10,11... | collective-permute-start | bytes 6291464 | tf_op jit(solution)/shard_map/ppermute | solution.py:57
  24.9 3.3 dynamic-slice_reduce_fusion.1
  40.9 6.0 %all-to-all-start.2 = ((bf16[8,4,512]{2,1,0:T(4,128)(2,1)}), bf16[8,4,512]{2,1,0:T(4,128)(2,1)S(1)}, u32[]{:S(2)}, u32[]{:S(2)}) async-start(bf16[8,4,512]{2,1,0:T(4,128)(2,1)} %broadcast_in_dim.123), calls=%async_computation.2 | async-start | bytes 65536 | tf_op jit(solution)/shard_map/all_to_all | solution.py:141
  46.9 23.0 %all-to-all-done.2 = bf16[8,4,512]{2,1,0:T(4,128)(2,1)S(1)} async-done(((bf16[8,4,512]{2,1,0:T(4,128)(2,1)}), bf16[8,4,512]{2,1,0:T(4,128)(2,1)S(1)}, u32[]{:S(2)}, u32[]{:S(2)}) %all-to-all-start.2) | async-done | bytes 32800 | tf_op jit(solution)/shard_map/all_to_all | solution.py:141
  77.2 5.7 %all-to-all-start.3 = ((bf16[8,4,512]{2,1,0:T(4,128)(2,1)}), bf16[8,4,512]{2,1,0:T(4,128)(2,1)S(1)}, u32[]{:S(2)}, u32[]{:S(2)}) async-start(bf16[8,4,512]{2,1,0:T(4,128)(2,1)} %broadcast_in_dim.124), calls=%async_computation.3 | async-start | bytes 65536 | tf_op jit(solution)/shard_map/all_to_all | solution.py:141
  82.9 5.8 %all_gather.15 = bf16[32,4096]{1,0:T(8,128)(2,1)S(1)} all-gather(bf16[8,4096]{1,0:T(8,128)(2,1)S(1)} %copy-done.10), channel_id=1, replica_groups=mesh['section'=4,'dp'=8] {'section'}, dimensions={0}, use_global_device_ids=true | all-gather | bytes 327680 | tf_op jit(solution)/shard_map/all_gather | solution.py:72
  92.8 5.2 %all-gather.1 = bf16[4,12,512]{2,1,0:T(8,128)(2,1)S(1)} all-gather(bf16[1,12,512]{2,1,0:T(8,128)(2,1)S(1)} %maximum_bitcast_fusion), channel_id=2, replica_groups=mesh['section'=4,'dp'=8] {'section'}, dimensions={0}, use_global_device_ids=true | all-gather | bytes 61440 | tf_op jit(solution)/shard_map/all_gather | solution.py:160
  98.7 5.1 %all-to-all-start.4 = ((bf16[8,12,512]{2,1,0:T(8,128)(2,1)}), bf16[8,12,512]{2,1,0:T(8,128)(2,1)S(1)}, u32[]{:S(2)}, u32[]{:S(2)}) async-start(bf16[8,12,512]{2,1,0:T(8,128)(2,1)} %broadcast_in_dim.126), calls=%async_computation.4 | async-start | bytes 262144 | tf_op jit(solution)/shard_map/all_to_all | solution.py:141
  105.0 3.9 %collective-permute-start.1 = (bf16[128,2048]{1,0:T(8,128)(2,1)S(1)}, bf16[128,2048]{1,0:T(8,128)(2,1)S(1)}, u32[]{:S(2)}, u32[]{:S(2)}) collective-permute-start(bf16[128,2048]{1,0:T(8,128)(2,1)S(1)} %maximum_select_fusion.2), channel_id=1, source_target_pairs={{0,2},{1,3},{2,0},{3,1},{4,6},{5,7},{6,4},{7,5},{16,18},{17,19},{1... | collective-permute-start | bytes 1572872 | tf_op jit(solution)/shard_map/ppermute | solution.py:57
  108.9 4.3 %collective-permute-start.2 = (bf16[128,2048]{1,0:T(8,128)(2,1)S(1)}, bf16[128,2048]{1,0:T(8,128)(2,1)S(1)}, u32[]{:S(2)}, u32[]{:S(2)}) collective-permute-start(bf16[128,2048]{1,0:T(8,128)(2,1)S(1)} %maximum_select_fusion.2), channel_id=1, source_target_pairs={{0,4},{1,5},{2,6},{3,7},{4,0},{5,1},{6,2},{7,3},{16,20},{17,21},{1... | collective-permute-start | bytes 1572872 | tf_op jit(solution)/shard_map/ppermute | solution.py:57
  115.1 6.0 %all-to-all-start = ((bf16[8,8,4224]{2,1,0:T(8,128)(2,1)}), bf16[8,8,4224]{2,1,0:T(8,128)(2,1)}, u32[]{:S(2)}, u32[]{:S(2)}) async-start(bf16[8,8,4224]{2,1,0:T(8,128)(2,1)} %pad_maximum_fusion.1), calls=%async_computation | async-start | bytes 1081344 | tf_op jit(solution)/shard_map/all_to_all | solution.py:71
  121.2 19.7 %collective-permute-done.2 = bf16[128,2048]{1,0:T(8,128)(2,1)S(1)} collective-permute-done((bf16[128,2048]{1,0:T(8,128)(2,1)S(1)}, bf16[128,2048]{1,0:T(8,128)(2,1)S(1)}, u32[]{:S(2)}, u32[]{:S(2)}) %collective-permute-start.2) | collective-permute-done | bytes 524320 | tf_op jit(solution)/shard_map/ppermute | solution.py:57
  144.0 3.6 %gather_fusion.2 = bf16[4,512,512]{2,1,0:T(8,128)(2,1)} fusion(bf16[4,512,512]{2,1,0:T(8,128)(2,1)} %collective-permute-done.6, s32[1024]{0:T(1024)S(1)} %pad_clamp_fusion.2), kind=kCustom, calls=%fused_computation.2.clone | custom fusion | bytes 4194320 | tf_op jit(solution)/shard_map/jit(_take)/gather | solution.py:84
  149.7 4.4 %convolution_convert_fusion.4 = bf16[512,512]{1,0:T(8,128)(2,1)S(1)} fusion(bf16[512,2048]{1,0:T(8,128)(2,1)} %get-tuple-element.16, bf16[2048,512]{1,0:T(8,128)(2,1)S(1)} %bitcast.204), kind=kOutput, calls=%fused_computation.46 | convolution fusion | flops 1074003968 | bytes 4718592 | tf_op jit(solution)/shard_map/dot_general | solution.py:98
  154.0 3.4 %collective-permute-start.7 = (bf16[512,512]{1,0:T(8,128)(2,1)S(1)}, bf16[512,512]{1,0:T(8,128)(2,1)S(1)}, u32[]{:S(2)}, u32[]{:S(2)}) collective-permute-start(bf16[512,512]{1,0:T(8,128)(2,1)S(1)} %convolution_convert_fusion.4), channel_id=1, source_target_pairs={{0,1},{1,0},{2,3},{3,2},{4,5},{5,4},{6,7},{7,6}} | collective-permute-start | bytes 1572872 | tf_op jit(solution)/shard_map/ppermute | solution.py:57
  159.9 5.2 %collective-permute-done.8 = f32[512]{0:T(512)S(1)} collective-permute-done((f32[512]{0:T(512)S(1)}, f32[512]{0:T(512)S(1)}, u32[]{:S(2)}, u32[]{:S(2)}) %collective-permute-start.8) | collective-permute-done | bytes 2080 | tf_op jit(solution)/shard_map/ppermute | solution.py:57
  175.1 7.4 %collective-permute-done.5 = bf16[512,2048]{1,0:T(8,128)(2,1)} collective-permute-done((bf16[512,2048]{1,0:T(8,128)(2,1)}, bf16[512,2048]{1,0:T(8,128)(2,1)}, u32[]{:S(2)}, u32[]{:S(2)}) %collective-permute-start.5) | collective-permute-done | bytes 2097184 | tf_op jit(solution)/shard_map/ppermute | solution.py:57
  183.8 4.5 %collective-permute-done.12 = bf16[512,512]{1,0:T(8,128)(2,1)S(1)} collective-permute-done((bf16[512,512]{1,0:T(8,128)(2,1)S(1)}, bf16[512,512]{1,0:T(8,128)(2,1)S(1)}, u32[]{:S(2)}, u32[]{:S(2)}) %collective-permute-start.12) | collective-permute-done | bytes 524320 | tf_op jit(solution)/shard_map/ppermute | solution.py:57
  192.7 3.4 %collective-permute-start.13 = (bf16[512,512]{1,0:T(8,128)(2,1)}, bf16[512,512]{1,0:T(8,128)(2,1)}, u32[]{:S(2)}, u32[]{:S(2)}) collective-permute-start(bf16[512,512]{1,0:T(8,128)(2,1)} %convolution_convert_fusion.3), channel_id=1, source_target_pairs={{0,1},{1,0},{2,3},{3,2},{4,5},{5,4},{6,7},{7,6},{8,9},{9,8},{10,11... | collective-permute-start | bytes 1572872 | tf_op jit(solution)/shard_map/ppermute | solution.py:57
  204.1 4.7 %add_convert_fusion.1 = bf16[512,512]{1,0:T(8,128)(2,1)} fusion(f32[512]{0:T(512)S(1)} %add_rsqrt_fusion.1, bf16[512,512]{1,0:T(8,128)(2,1)} %collective-permute-done.13, bf16[512,2048]{1,0:T(8,128)(2,1)} %copy-done.2, bf16[2048,512]{1,0:T(8,128)(2,1)} %bitcast.202, s32[]{:T(128)S(6)} %select_n.252), kind=kOutput, calls=%fused_computation.64 | convolution fusion | flops 1076887552 | bytes 5769220 | tf_op jit(solution)/shard_map/dot_general | solution.py:100
  212.5 9.0 %collective-permute-start.15 = (bf16[512,512]{1,0:T(8,128)(2,1)S(1)}, bf16[512,512]{1,0:T(8,128)(2,1)S(1)}, u32[]{:S(2)}, u32[]{:S(2)}) collective-permute-start(bf16[512,512]{1,0:T(8,128)(2,1)S(1)} %bitcast_select_fusion.2), channel_id=1, source_target_pairs={{0,8},{1,9},{2,10},{3,11},{4,12},{5,13},{6,14},{7,15},{8,16},{9,17... | collective-permute-start | bytes 1572872 | tf_op jit(solution)/shard_map/ppermute | solution.py:57
  221.5 13.5 %collective-permute-start.16 = (bf16[512,512]{1,0:T(8,128)(2,1)S(1)}, bf16[512,512]{1,0:T(8,128)(2,1)S(1)}, u32[]{:S(2)}, u32[]{:S(2)}) collective-permute-start(bf16[512,512]{1,0:T(8,128)(2,1)S(1)} %bitcast_select_fusion.2), channel_id=1, source_target_pairs={{0,10},{1,11},{2,8},{3,9},{4,14},{5,15},{6,12},{7,13},{8,18},{9,19... | collective-permute-start | bytes 1572872 | tf_op jit(solution)/shard_map/ppermute | solution.py:57
  238.5 7.8 %collective-permute-done.16 = bf16[512,512]{1,0:T(8,128)(2,1)S(1)} collective-permute-done((bf16[512,512]{1,0:T(8,128)(2,1)S(1)}, bf16[512,512]{1,0:T(8,128)(2,1)S(1)}, u32[]{:S(2)}, u32[]{:S(2)}) %collective-permute-start.16) | collective-permute-done | bytes 524320 | tf_op jit(solution)/shard_map/ppermute | solution.py:57
  246.3 5.7 %collective-permute-done.17 = bf16[512,512]{1,0:T(8,128)(2,1)S(1)} collective-permute-done((bf16[512,512]{1,0:T(8,128)(2,1)S(1)}, bf16[512,512]{1,0:T(8,128)(2,1)S(1)}, u32[]{:S(2)}, u32[]{:S(2)}) %collective-permute-start.17) | collective-permute-done | bytes 524320 | tf_op jit(solution)/shard_map/ppermute | solution.py:57
  251.9 5.7 %collective-permute-done.18 = bf16[512,512]{1,0:T(8,128)(2,1)S(1)} collective-permute-done((bf16[512,512]{1,0:T(8,128)(2,1)S(1)}, bf16[512,512]{1,0:T(8,128)(2,1)S(1)}, u32[]{:S(2)}, u32[]{:S(2)}) %collective-permute-start.18) | collective-permute-done | bytes 524320 | tf_op jit(solution)/shard_map/ppermute | solution.py:57
  259.9 3.4 %collective-permute-start.19 = (bf16[512,512]{1,0:T(8,128)(2,1)S(1)}, bf16[512,512]{1,0:T(8,128)(2,1)S(1)}, u32[]{:S(2)}, u32[]{:S(2)}) collective-permute-start(bf16[512,512]{1,0:T(8,128)(2,1)S(1)} %convolution_convert_fusion.2), channel_id=1, source_target_pairs={{0,1},{1,0},{2,3},{3,2},{4,5},{5,4},{6,7},{7,6},{8,9},{9,8},{10,11... | collective-permute-start | bytes 1572872 | tf_op jit(solution)/shard_map/ppermute | solution.py:57
  266.6 17.0 %all_gather.14 = f32[32,64]{1,0:T(8,128)S(1)} all-gather(f32[8,64]{1,0:T(8,128)S(1)} %select_reduce_fusion), channel_id=1, replica_groups=mesh['section'=4,'dp'=8] {'section'}, dimensions={0}, use_global_device_ids=true | all-gather | bytes 10240 | tf_op jit(solution)/shard_map/all_gather | solution.py:191
  289.1 12.7 %all-to-all-start.5 = ((bf16[8,8,4096]{2,1,0:T(8,128)(2,1)}), bf16[8,8,4096]{2,1,0:T(8,128)(2,1)S(1)}, u32[]{:S(2)}, u32[]{:S(2)}) async-start(bf16[8,8,4096]{2,1,0:T(8,128)(2,1)} %fusion.2), calls=%async_computation.5 | async-start | bytes 1048576 | tf_op jit(solution)/shard_map/all_to_all | solution.py:196
  307.7 3.8 %collective-permute-start.26 = (bf16[64,512]{1,0:T(8,128)(2,1)S(1)}, bf16[64,512]{1,0:T(8,128)(2,1)S(1)}, u32[]{:S(2)}, u32[]{:S(2)}) collective-permute-start(bf16[64,512]{1,0:T(8,128)(2,1)S(1)} %get-tuple-element.20), channel_id=1, source_target_pairs={{0,6},{1,7},{2,4},{3,5},{4,2},{5,3},{6,0},{7,1},{8,14},{9,15},{10,... | collective-permute-start | bytes 196616 | tf_op jit(solution)/shard_map/ppermute | solution.py:40
  313.3 4.4 %collective-permute-start.27 = (bf16[64,512]{1,0:T(8,128)(2,1)S(1)}, bf16[64,512]{1,0:T(8,128)(2,1)S(1)}, u32[]{:S(2)}, u32[]{:S(2)}) collective-permute-start(bf16[64,512]{1,0:T(8,128)(2,1)S(1)} %get-tuple-element.19), channel_id=1, source_target_pairs={{0,7},{1,6},{2,5},{3,4},{4,3},{5,2},{6,1},{7,0},{8,15},{9,14},{10,... | collective-permute-start | bytes 196616 | tf_op jit(solution)/shard_map/ppermute | solution.py:40
  317.8 6.9 %collective-permute-done.24 = bf16[64,512]{1,0:T(8,128)(2,1)S(1)} collective-permute-done((bf16[64,512]{1,0:T(8,128)(2,1)S(1)}, bf16[64,512]{1,0:T(8,128)(2,1)S(1)}, u32[]{:S(2)}, u32[]{:S(2)}) %collective-permute-start.24) | collective-permute-done | bytes 65568 | tf_op jit(solution)/shard_map/ppermute | solution.py:40
  (206 shorter events, 105.5 us)
Async XLA Ops:
  3.9 30.9 %all-to-all-start.1 = ((bf16[8,2,2048]{2,1,0:T(2,128)(2,1)}), bf16[8,2,2048]{2,1,0:T(2,128)(2,1)S(1)}, u32[]{:S(2)}, u32[]{:S(2)}) async-start(bf16[8,2,2048]{2,1,0:T(2,128)(2,1)} %reshape.403), calls=%async_computation.1 | async-start | bytes 131072 | tf_op jit(solution)/shard_map/all_to_all | solution.py:141
  17.5 126.5 %collective-permute-start.6 = (bf16[4,512,512]{2,1,0:T(8,128)(2,1)}, bf16[4,512,512]{2,1,0:T(8,128)(2,1)}, u32[]{:S(2)}, u32[]{:S(2)}) collective-permute-start(bf16[4,512,512]{2,1,0:T(8,128)(2,1)} %get-tuple-element.18), channel_id=1, source_target_pairs={{0,1},{1,0},{2,3},{3,2},{4,5},{5,4},{6,7},{7,6},{8,9},{9,8},{10,11... | collective-permute-start | bytes 6291464 | tf_op jit(solution)/shard_map/ppermute | solution.py:57
  29.0 74.8 %collective-permute-start = (bf16[64,2048]{1,0:T(8,128)(2,1)}, bf16[64,2048]{1,0:T(8,128)(2,1)}, u32[]{:S(2)}, u32[]{:S(2)}) collective-permute-start(bf16[64,2048]{1,0:T(8,128)(2,1)} %bitcast.53), channel_id=1, source_target_pairs={{0,1},{1,0},{2,3},{3,2},{4,5},{5,4},{6,7},{7,6},{16,17},{17,16},{1... | collective-permute-start | bytes 786440 | tf_op jit(solution)/shard_map/ppermute | solution.py:57
  40.9 29.0 %all-to-all-start.2 = ((bf16[8,4,512]{2,1,0:T(4,128)(2,1)}), bf16[8,4,512]{2,1,0:T(4,128)(2,1)S(1)}, u32[]{:S(2)}, u32[]{:S(2)}) async-start(bf16[8,4,512]{2,1,0:T(4,128)(2,1)} %broadcast_in_dim.123), calls=%async_computation.2 | async-start | bytes 65536 | tf_op jit(solution)/shard_map/all_to_all | solution.py:141
  77.2 12.4 %all-to-all-start.3 = ((bf16[8,4,512]{2,1,0:T(4,128)(2,1)}), bf16[8,4,512]{2,1,0:T(4,128)(2,1)S(1)}, u32[]{:S(2)}, u32[]{:S(2)}) async-start(bf16[8,4,512]{2,1,0:T(4,128)(2,1)} %broadcast_in_dim.124), calls=%async_computation.3 | async-start | bytes 65536 | tf_op jit(solution)/shard_map/all_to_all | solution.py:141
  98.7 16.4 %all-to-all-start.4 = ((bf16[8,12,512]{2,1,0:T(8,128)(2,1)}), bf16[8,12,512]{2,1,0:T(8,128)(2,1)S(1)}, u32[]{:S(2)}, u32[]{:S(2)}) async-start(bf16[8,12,512]{2,1,0:T(8,128)(2,1)} %broadcast_in_dim.126), calls=%async_computation.4 | async-start | bytes 262144 | tf_op jit(solution)/shard_map/all_to_all | solution.py:141
  105.0 16.2 %collective-permute-start.1 = (bf16[128,2048]{1,0:T(8,128)(2,1)S(1)}, bf16[128,2048]{1,0:T(8,128)(2,1)S(1)}, u32[]{:S(2)}, u32[]{:S(2)}) collective-permute-start(bf16[128,2048]{1,0:T(8,128)(2,1)S(1)} %maximum_select_fusion.2), channel_id=1, source_target_pairs={{0,2},{1,3},{2,0},{3,1},{4,6},{5,7},{6,4},{7,5},{16,18},{17,19},{1... | collective-permute-start | bytes 1572872 | tf_op jit(solution)/shard_map/ppermute | solution.py:57
  108.9 31.9 %collective-permute-start.2 = (bf16[128,2048]{1,0:T(8,128)(2,1)S(1)}, bf16[128,2048]{1,0:T(8,128)(2,1)S(1)}, u32[]{:S(2)}, u32[]{:S(2)}) collective-permute-start(bf16[128,2048]{1,0:T(8,128)(2,1)S(1)} %maximum_select_fusion.2), channel_id=1, source_target_pairs={{0,4},{1,5},{2,6},{3,7},{4,0},{5,1},{6,2},{7,3},{16,20},{17,21},{1... | collective-permute-start | bytes 1572872 | tf_op jit(solution)/shard_map/ppermute | solution.py:57
  113.2 27.7 %collective-permute-start.3 = (bf16[128,2048]{1,0:T(8,128)(2,1)S(1)}, bf16[128,2048]{1,0:T(8,128)(2,1)S(1)}, u32[]{:S(2)}, u32[]{:S(2)}) collective-permute-start(bf16[128,2048]{1,0:T(8,128)(2,1)S(1)} %maximum_select_fusion.2), channel_id=1, source_target_pairs={{0,6},{1,7},{2,4},{3,5},{4,2},{5,3},{6,0},{7,1},{16,22},{17,23},{1... | collective-permute-start | bytes 1572872 | tf_op jit(solution)/shard_map/ppermute | solution.py:57
  115.1 81.0 %all-to-all-start = ((bf16[8,8,4224]{2,1,0:T(8,128)(2,1)}), bf16[8,8,4224]{2,1,0:T(8,128)(2,1)}, u32[]{:S(2)}, u32[]{:S(2)}) async-start(bf16[8,8,4224]{2,1,0:T(8,128)(2,1)} %pad_maximum_fusion.1), calls=%async_computation | async-start | bytes 1081344 | tf_op jit(solution)/shard_map/all_to_all | solution.py:71
  142.4 40.1 %collective-permute-start.5 = (bf16[512,2048]{1,0:T(8,128)(2,1)}, bf16[512,2048]{1,0:T(8,128)(2,1)}, u32[]{:S(2)}, u32[]{:S(2)}) collective-permute-start(bf16[512,2048]{1,0:T(8,128)(2,1)} %get-tuple-element.16), channel_id=1, source_target_pairs={{16,0},{17,1},{18,2},{19,3},{20,4},{21,5},{22,6},{23,7}} | collective-permute-start | bytes 6291464 | tf_op jit(solution)/shard_map/ppermute | solution.py:57
  154.0 11.1 %collective-permute-start.7 = (bf16[512,512]{1,0:T(8,128)(2,1)S(1)}, bf16[512,512]{1,0:T(8,128)(2,1)S(1)}, u32[]{:S(2)}, u32[]{:S(2)}) collective-permute-start(bf16[512,512]{1,0:T(8,128)(2,1)S(1)} %convolution_convert_fusion.4), channel_id=1, source_target_pairs={{0,1},{1,0},{2,3},{3,2},{4,5},{5,4},{6,7},{7,6}} | collective-permute-start | bytes 1572872 | tf_op jit(solution)/shard_map/ppermute | solution.py:57
  169.1 14.7 %collective-permute-start.10 = (bf16[512,512]{1,0:T(8,128)(2,1)S(1)}, bf16[512,512]{1,0:T(8,128)(2,1)S(1)}, u32[]{:S(2)}, u32[]{:S(2)}) collective-permute-start(bf16[512,512]{1,0:T(8,128)(2,1)S(1)} %bitcast.210), channel_id=1, source_target_pairs={{0,10},{1,11},{2,8},{3,9},{4,14},{5,15},{6,12},{7,13}} | collective-permute-start | bytes 1572872 | tf_op jit(solution)/shard_map/ppermute | solution.py:57
  170.4 13.4 %collective-permute-start.11 = (bf16[512,512]{1,0:T(8,128)(2,1)S(1)}, bf16[512,512]{1,0:T(8,128)(2,1)S(1)}, u32[]{:S(2)}, u32[]{:S(2)}) collective-permute-start(bf16[512,512]{1,0:T(8,128)(2,1)S(1)} %bitcast.211), channel_id=1, source_target_pairs={{0,12},{1,13},{2,14},{3,15},{4,8},{5,9},{6,10},{7,11}} | collective-permute-start | bytes 1572872 | tf_op jit(solution)/shard_map/ppermute | solution.py:57
  171.8 16.6 %collective-permute-start.12 = (bf16[512,512]{1,0:T(8,128)(2,1)S(1)}, bf16[512,512]{1,0:T(8,128)(2,1)S(1)}, u32[]{:S(2)}, u32[]{:S(2)}) collective-permute-start(bf16[512,512]{1,0:T(8,128)(2,1)S(1)} %bitcast.212), channel_id=1, source_target_pairs={{0,14},{1,15},{2,12},{3,13},{4,10},{5,11},{6,8},{7,9}} | collective-permute-start | bytes 1572872 | tf_op jit(solution)/shard_map/ppermute | solution.py:57
  173.1 15.3 %collective-permute-start.9 = (bf16[512,512]{1,0:T(8,128)(2,1)S(1)}, bf16[512,512]{1,0:T(8,128)(2,1)S(1)}, u32[]{:S(2)}, u32[]{:S(2)}) collective-permute-start(bf16[512,512]{1,0:T(8,128)(2,1)S(1)} %bitcast.213), channel_id=1, source_target_pairs={{0,8},{1,9},{2,10},{3,11},{4,12},{5,13},{6,14},{7,15}} | collective-permute-start | bytes 1572872 | tf_op jit(solution)/shard_map/ppermute | solution.py:57
  182.5 55.9 %collective-permute-start.4 = (bf16[512,2048]{1,0:T(8,128)(2,1)}, bf16[512,2048]{1,0:T(8,128)(2,1)S(1)}, u32[]{:S(2)}, u32[]{:S(2)}) collective-permute-start(bf16[512,2048]{1,0:T(8,128)(2,1)} %get-tuple-element.16), channel_id=1, source_target_pairs={{24,0},{25,1},{26,2},{27,3},{28,4},{29,5},{30,6},{31,7}} | collective-permute-start | bytes 6291464 | tf_op jit(solution)/shard_map/ppermute | solution.py:57
  192.7 11.4 %collective-permute-start.13 = (bf16[512,512]{1,0:T(8,128)(2,1)}, bf16[512,512]{1,0:T(8,128)(2,1)}, u32[]{:S(2)}, u32[]{:S(2)}) collective-permute-start(bf16[512,512]{1,0:T(8,128)(2,1)} %convolution_convert_fusion.3), channel_id=1, source_target_pairs={{0,1},{1,0},{2,3},{3,2},{4,5},{5,4},{6,7},{7,6},{8,9},{9,8},{10,11... | collective-permute-start | bytes 1572872 | tf_op jit(solution)/shard_map/ppermute | solution.py:57
  212.5 25.9 %collective-permute-start.15 = (bf16[512,512]{1,0:T(8,128)(2,1)S(1)}, bf16[512,512]{1,0:T(8,128)(2,1)S(1)}, u32[]{:S(2)}, u32[]{:S(2)}) collective-permute-start(bf16[512,512]{1,0:T(8,128)(2,1)S(1)} %bitcast_select_fusion.2), channel_id=1, source_target_pairs={{0,8},{1,9},{2,10},{3,11},{4,12},{5,13},{6,14},{7,15},{8,16},{9,17... | collective-permute-start | bytes 1572872 | tf_op jit(solution)/shard_map/ppermute | solution.py:57
  221.5 24.8 %collective-permute-start.16 = (bf16[512,512]{1,0:T(8,128)(2,1)S(1)}, bf16[512,512]{1,0:T(8,128)(2,1)S(1)}, u32[]{:S(2)}, u32[]{:S(2)}) collective-permute-start(bf16[512,512]{1,0:T(8,128)(2,1)S(1)} %bitcast_select_fusion.2), channel_id=1, source_target_pairs={{0,10},{1,11},{2,8},{3,9},{4,14},{5,15},{6,12},{7,13},{8,18},{9,19... | collective-permute-start | bytes 1572872 | tf_op jit(solution)/shard_map/ppermute | solution.py:57
  235.1 16.9 %collective-permute-start.17 = (bf16[512,512]{1,0:T(8,128)(2,1)S(1)}, bf16[512,512]{1,0:T(8,128)(2,1)S(1)}, u32[]{:S(2)}, u32[]{:S(2)}) collective-permute-start(bf16[512,512]{1,0:T(8,128)(2,1)S(1)} %bitcast_select_fusion.2), channel_id=1, source_target_pairs={{0,12},{1,13},{2,14},{3,15},{4,8},{5,9},{6,10},{7,11},{8,20},{9,21... | collective-permute-start | bytes 1572872 | tf_op jit(solution)/shard_map/ppermute | solution.py:57
  236.4 21.2 %collective-permute-start.18 = (bf16[512,512]{1,0:T(8,128)(2,1)S(1)}, bf16[512,512]{1,0:T(8,128)(2,1)S(1)}, u32[]{:S(2)}, u32[]{:S(2)}) collective-permute-start(bf16[512,512]{1,0:T(8,128)(2,1)S(1)} %bitcast_select_fusion.2), channel_id=1, source_target_pairs={{0,14},{1,15},{2,12},{3,13},{4,10},{5,11},{6,8},{7,9},{8,22},{9,23... | collective-permute-start | bytes 1572872 | tf_op jit(solution)/shard_map/ppermute | solution.py:57
  259.9 23.8 %collective-permute-start.19 = (bf16[512,512]{1,0:T(8,128)(2,1)S(1)}, bf16[512,512]{1,0:T(8,128)(2,1)S(1)}, u32[]{:S(2)}, u32[]{:S(2)}) collective-permute-start(bf16[512,512]{1,0:T(8,128)(2,1)S(1)} %convolution_convert_fusion.2), channel_id=1, source_target_pairs={{0,1},{1,0},{2,3},{3,2},{4,5},{5,4},{6,7},{7,6},{8,9},{9,8},{10,11... | collective-permute-start | bytes 1572872 | tf_op jit(solution)/shard_map/ppermute | solution.py:57
  264.2 19.5 %collective-permute-start.20 = (f32[512]{0:T(512)S(1)}, f32[512]{0:T(512)S(1)}, u32[]{:S(2)}, u32[]{:S(2)}) collective-permute-start(f32[512]{0:T(512)S(1)} %get-tuple-element.11), channel_id=1, source_target_pairs={{0,1},{1,0},{2,3},{3,2},{4,5},{5,4},{6,7},{7,6},{8,9},{9,8},{10,11... | collective-permute-start | bytes 6152 | tf_op jit(solution)/shard_map/ppermute | solution.py:57
  286.1 21.6 %collective-permute-start.21 = (bf16[64,512]{1,0:T(8,128)(2,1)S(1)}, bf16[64,512]{1,0:T(8,128)(2,1)S(1)}, u32[]{:S(2)}, u32[]{:S(2)}) collective-permute-start(bf16[64,512]{1,0:T(8,128)(2,1)S(1)} %get-tuple-element.25), channel_id=1, source_target_pairs={{0,1},{1,0},{2,3},{3,2},{4,5},{5,4},{6,7},{7,6},{8,9},{9,8},{10,11... | collective-permute-start | bytes 196616 | tf_op jit(solution)/shard_map/ppermute | solution.py:40
  289.1 40.0 %all-to-all-start.5 = ((bf16[8,8,4096]{2,1,0:T(8,128)(2,1)}), bf16[8,8,4096]{2,1,0:T(8,128)(2,1)S(1)}, u32[]{:S(2)}, u32[]{:S(2)}) async-start(bf16[8,8,4096]{2,1,0:T(8,128)(2,1)} %fusion.2), calls=%async_computation.5 | async-start | bytes 1048576 | tf_op jit(solution)/shard_map/all_to_all | solution.py:196
  301.8 11.5 %collective-permute-start.22 = (bf16[64,512]{1,0:T(8,128)(2,1)S(1)}, bf16[64,512]{1,0:T(8,128)(2,1)S(1)}, u32[]{:S(2)}, u32[]{:S(2)}) collective-permute-start(bf16[64,512]{1,0:T(8,128)(2,1)S(1)} %get-tuple-element.24), channel_id=1, source_target_pairs={{0,2},{1,3},{2,0},{3,1},{4,6},{5,7},{6,4},{7,5},{8,10},{9,11},{10,... | collective-permute-start | bytes 196616 | tf_op jit(solution)/shard_map/ppermute | solution.py:40
  303.8 13.9 %collective-permute-start.23 = (bf16[64,512]{1,0:T(8,128)(2,1)S(1)}, bf16[64,512]{1,0:T(8,128)(2,1)S(1)}, u32[]{:S(2)}, u32[]{:S(2)}) collective-permute-start(bf16[64,512]{1,0:T(8,128)(2,1)S(1)} %get-tuple-element.23), channel_id=1, source_target_pairs={{0,3},{1,2},{2,1},{3,0},{4,7},{5,6},{6,5},{7,4},{8,11},{9,10},{10,... | collective-permute-start | bytes 196616 | tf_op jit(solution)/shard_map/ppermute | solution.py:40
  305.3 19.4 %collective-permute-start.24 = (bf16[64,512]{1,0:T(8,128)(2,1)S(1)}, bf16[64,512]{1,0:T(8,128)(2,1)S(1)}, u32[]{:S(2)}, u32[]{:S(2)}) collective-permute-start(bf16[64,512]{1,0:T(8,128)(2,1)S(1)} %get-tuple-element.22), channel_id=1, source_target_pairs={{0,4},{1,5},{2,6},{3,7},{4,0},{5,1},{6,2},{7,3},{8,12},{9,13},{10,... | collective-permute-start | bytes 196616 | tf_op jit(solution)/shard_map/ppermute | solution.py:40
  307.7 19.0 %collective-permute-start.25 = (bf16[64,512]{1,0:T(8,128)(2,1)S(1)}, bf16[64,512]{1,0:T(8,128)(2,1)S(1)}, u32[]{:S(2)}, u32[]{:S(2)}) collective-permute-start(bf16[64,512]{1,0:T(8,128)(2,1)S(1)} %get-tuple-element.21), channel_id=1, source_target_pairs={{0,5},{1,4},{2,7},{3,6},{4,1},{5,0},{6,3},{7,2},{8,13},{9,12},{10,... | collective-permute-start | bytes 196616 | tf_op jit(solution)/shard_map/ppermute | solution.py:40
  307.7 19.0 %collective-permute-start.26 = (bf16[64,512]{1,0:T(8,128)(2,1)S(1)}, bf16[64,512]{1,0:T(8,128)(2,1)S(1)}, u32[]{:S(2)}, u32[]{:S(2)}) collective-permute-start(bf16[64,512]{1,0:T(8,128)(2,1)S(1)} %get-tuple-element.20), channel_id=1, source_target_pairs={{0,6},{1,7},{2,4},{3,5},{4,2},{5,3},{6,0},{7,1},{8,14},{9,15},{10,... | collective-permute-start | bytes 196616 | tf_op jit(solution)/shard_map/ppermute | solution.py:40
  313.3 13.4 %collective-permute-start.27 = (bf16[64,512]{1,0:T(8,128)(2,1)S(1)}, bf16[64,512]{1,0:T(8,128)(2,1)S(1)}, u32[]{:S(2)}, u32[]{:S(2)}) collective-permute-start(bf16[64,512]{1,0:T(8,128)(2,1)S(1)} %get-tuple-element.19), channel_id=1, source_target_pairs={{0,7},{1,6},{2,5},{3,4},{4,3},{5,2},{6,1},{7,0},{8,15},{9,14},{10,... | collective-permute-start | bytes 196616 | tf_op jit(solution)/shard_map/ppermute | solution.py:40
  (21 other events, 205.2 us)
